TPU v7x, 512 devices: a whole 4x8x8 slice. The times are simulated.
512 devices in a mesh: row: 32 (over x, y), col: 8 (over z_hi, core), vec: 2 (over z_lo).
Axes of the slice: x: 4, y: 8, z: 8 (z_hi: 4, z_lo: 2; z = z_hi * 2 + z_lo), core: 2. Of those that a mesh axis runs over, the one named last changes fastest.
Arguments:
- vectors: bfloat16 [131072, 256], P(('row', 'col'), 'vec'), parts along dimension 1, may hold values from -6 to 6
- tile_blocks: bfloat16 [32, 8, 32, 256, 256], P('row', 'col'), may hold values from -0.125 to 0.125
- block_rows: int32 [32, 8, 32], P('row', 'col'), may hold values from 0 to 15, as said below
- block_cols: int32 [32, 8, 32], P('row', 'col'), may hold values from 0 to 63, as said below
- counts: int32 [32, 8], P('row', 'col'), may hold values from 1 to 32, as said below
Outputs:
- filtered: bfloat16 [131072, 256], P(('row', 'col'), 'vec'), parts along dimension 1
There are 2 independent parts, one for each index of `vec`. A program takes and returns all parts, laid end to end along the dimension named above; an argument that names none is the same for every part. Nothing has to cross between parts.
Inputs may be any that keep to these rules, and one draw needn't show every extreme that they name: The pairs (block_rows, block_cols // 2) of the 32 slots of one tile are all distinct. Within one tile, all slots whose block columns lie in the same group of 2 (same block_cols // 2) name the same block column. `counts`: some tile uses all 32 slots.
All inputs are finite; a program needn't handle non-finite values.
Results may differ from a plain program's by a relative error of at most 0.015.
Values may be sent and summed in bfloat16 or wider, within the bound.
A program may use at most 64 MiB of HBM per device.

v0:
```python
import jax
import jax.numpy as jnp
from jax import lax
from jax.sharding import PartitionSpec as P

DEGREE = 3


center_value = 0.5
half_width = 2.0


def on_device(vectors, tile_blocks, block_rows, block_cols, counts):
    n_row = lax.axis_size("row")
    n_col = lax.axis_size("col")
    tile_data = tile_blocks[0, 0]
    slot_rows = block_rows[0, 0]
    slot_cols = block_cols[0, 0]
    used = counts[0, 0]
    block_size = tile_data.shape[-1]
    width = vectors.shape[1]
    piece_blocks = vectors.shape[0] // block_size
    row_blocks = piece_blocks * n_col
    slot_count = tile_data.shape[0]
    live = (jnp.arange(slot_count) < used).astype(jnp.float32)
    onehot = (slot_rows[None, :] == jnp.arange(row_blocks)[:, None]).astype(jnp.float32) * live[
        None, :
    ]

    def apply_tiles(current):
        gathered = lax.all_gather(current, "row", axis=0, tiled=True)
        vec_blocks = jnp.take(
            gathered.reshape(n_row * piece_blocks, block_size, width), slot_cols, axis=0
        )
        products = jnp.einsum(
            "sij,sjk->sik", tile_data, vec_blocks, preferred_element_type=jnp.float32
        )
        term = jnp.einsum("ls,sik->lik", onehot, products, precision=lax.Precision.HIGHEST)
        term = term.reshape(row_blocks * block_size, width)
        return lax.psum_scatter(
            term.astype(jnp.bfloat16), "col", scatter_dimension=0, tiled=True
        ).astype(jnp.float32)

    previous = vectors
    applied = apply_tiles(vectors)
    current = ((applied - center_value * previous.astype(jnp.float32)) / half_width).astype(
        jnp.bfloat16
    )
    for repeat in range(DEGREE - 1):
        applied = apply_tiles(current)
        following = (
            2.0 * (applied - center_value * current.astype(jnp.float32)) / half_width
            - previous.astype(jnp.float32)
        ).astype(jnp.bfloat16)
        previous, current = (current, following)
    return current


def solution(mesh):
    return jax.shard_map(
        on_device,
        mesh=mesh,
        in_specs=(
            P(("row", "col"), "vec"),
            P("row", "col", None, None, None),
            P("row", "col", None),
            P("row", "col", None),
            P("row", "col"),
        ),
        out_specs=P(("row", "col"), "vec"),
        check_vma=False,
    )
```

profile of v0, /device:TPU:1, one launch (start us, length us, event | category | flops | bytes accessed | tf_op | source)
XLA Modules:
  0.0 469.2 jit_solution(5632547068831693479)
XLA Ops:
  9.3 90.2 %all-gather.4.cloned.1.call-done = bf16[16384,128]{1,0:T(8,128)(2,1)} async-done(((bf16[512,128]{1,0:T(8,128)(2,1)}), bf16[16384,128]{1,0:T(8,128)(2,1)}) %all-gather.4.cloned.1.call-update) | async-done | bytes 4194320 | tf_op jit(solution)/shard_map/all_gather | solution.py:31
  99.5 3.1 gather_fusion
  102.6 6.6 %fusion.10 = f32[32,128,256]{2,1,0:T(8,128)} fusion(bf16[1,1,32,256,256]{4,3,2,1,0:T(8,128)(2,1)} %param.8, bf16[32,256,128]{2,1,0:T(8,128)(2,1)S(1)} %gather_fusion, pred[32]{0:T(512)(128)(4,1)S(1)} %compare_and_fusion), kind=kOutput, calls=%fused_computation.13 | convolution fusion | flops 537919488 | bytes 10485792 | tf_op jit(solution)/shard_map/sij,sjk->sik/dot_general | solution.py:35
  109.2 5.5 %copy.9 = f32[32,128,256]{1,0,2:T(8,128)} copy(f32[32,128,256]{2,1,0:T(8,128)} %fusion.10) | data formatting | bytes 8388608 | tf_op jit(solution)/shard_map/sij,sjk->sik/dot_general | solution.py:35
  114.7 4.3 fusion.18
  119.0 1.2 copy.6
  120.4 42.3 %reduce-scatter.4.cloned.1.call-done = bf16[512,128]{1,0:T(8,128)(2,1)} async-done(((bf16[4096,128]{1,0:T(8,128)(2,1)}), bf16[512,128]{1,0:T(8,128)(2,1)}) %reduce-scatter.4.cloned.1.call-update) | async-done | bytes 131088 | tf_op jit(solution)/shard_map/reduce_scatter | solution.py:40
  162.6 1.6 fusion.32
  164.3 84.2 %all-gather.6.cloned.1.call-done = bf16[16384,128]{1,0:T(8,128)(2,1)} async-done(((bf16[512,128]{1,0:T(8,128)(2,1)}), bf16[16384,128]{1,0:T(8,128)(2,1)}) %all-gather.6.cloned.1.call-update) | async-done | bytes 4194320 | tf_op jit(solution)/shard_map/all_gather | solution.py:31
  248.6 3.1 gather_fusion.1
  251.7 6.6 %fusion.8 = f32[32,128,256]{2,1,0:T(8,128)} fusion(bf16[1,1,32,256,256]{4,3,2,1,0:T(8,128)(2,1)} %param.8, bf16[32,256,128]{2,1,0:T(8,128)(2,1)S(1)} %gather_fusion.1, pred[32]{0:T(512)(128)(4,1)S(1)} %compare_and_fusion), kind=kOutput, calls=%fused_computation.11 | convolution fusion | flops 537919488 | bytes 10485792 | tf_op jit(solution)/shard_map/sij,sjk->sik/dot_general | solution.py:35
  258.3 5.5 %copy.10 = f32[32,128,256]{1,0,2:T(8,128)} copy(f32[32,128,256]{2,1,0:T(8,128)} %fusion.8) | data formatting | bytes 8388608 | tf_op jit(solution)/shard_map/sij,sjk->sik/dot_general | solution.py:35
  263.8 4.3 fusion.21
  268.1 1.2 copy.7
  269.4 42.4 %reduce-scatter.6.cloned.1.call-done = bf16[512,128]{1,0:T(8,128)(2,1)} async-done(((bf16[4096,128]{1,0:T(8,128)(2,1)}), bf16[512,128]{1,0:T(8,128)(2,1)}) %reduce-scatter.6.cloned.1.call-update) | async-done | bytes 131088 | tf_op jit(solution)/shard_map/reduce_scatter | solution.py:40
  311.8 1.6 fusion.33
  313.7 83.9 %all-gather.8.cloned.1.call-done = bf16[16384,128]{1,0:T(8,128)(2,1)} async-done(((bf16[512,128]{1,0:T(8,128)(2,1)}), bf16[16384,128]{1,0:T(8,128)(2,1)}) %all-gather.8.cloned.1.call-update) | async-done | bytes 4194320 | tf_op jit(solution)/shard_map/all_gather | solution.py:31
  397.6 3.1 gather_fusion.2
  400.7 6.6 %fusion.6 = f32[32,128,256]{2,1,0:T(8,128)} fusion(bf16[1,1,32,256,256]{4,3,2,1,0:T(8,128)(2,1)} %param.8, bf16[32,256,128]{2,1,0:T(8,128)(2,1)S(1)} %gather_fusion.2, pred[32]{0:T(512)(128)(4,1)S(1)} %compare_and_fusion), kind=kOutput, calls=%fused_computation.9 | convolution fusion | flops 537919488 | bytes 10485792 | tf_op jit(solution)/shard_map/sij,sjk->sik/dot_general | solution.py:35
  407.3 5.5 %copy.11 = f32[32,128,256]{1,0,2:T(8,128)} copy(f32[32,128,256]{2,1,0:T(8,128)} %fusion.6) | data formatting | bytes 8388608 | tf_op jit(solution)/shard_map/sij,sjk->sik/dot_general | solution.py:35
  412.8 4.3 fusion.24
  417.1 1.2 copy.8
  418.4 42.3 %reduce-scatter.8.cloned.1.call-done = bf16[512,128]{1,0:T(8,128)(2,1)} async-done(((bf16[4096,128]{1,0:T(8,128)(2,1)}), bf16[512,128]{1,0:T(8,128)(2,1)}) %reduce-scatter.8.cloned.1.call-update) | async-done | bytes 131088 | tf_op jit(solution)/shard_map/reduce_scatter | solution.py:40
  460.7 1.6 fusion.35
  (24 shorter events, 2.5 us)
Async XLA Ops:
  6.5 93.0 %all-gather.4.cloned.1.call-start = ((), (), s32[]{:S(2)}) async-start(), calls=%async_computation.3 | async-start | bytes 4325376 | tf_op jit(solution)/shard_map/all_gather | solution.py:31
  7.3 155.4 %reduce-scatter.4.cloned.1.call-start = ((), (), s32[]{:S(2)}) async-start(), calls=%async_computation.4 | async-start | bytes 1179648 | tf_op jit(solution)/shard_map/reduce_scatter | solution.py:40
  109.2 5.5 %copy-start.3 = (s32[1,1,32]{2,1,0:T(1,128)S(1)}, s32[1,1,32]{2,1,0:T(1,128)}, u32[]{:S(2)}) copy-start(s32[1,1,32]{2,1,0:T(1,128)} %param.9) | copy-start | bytes 388
  114.7 47.9 %copy-start.1 = (bf16[512,128]{1,0:T(8,128)(2,1)S(1)}, bf16[512,128]{1,0:T(8,128)(2,1)}, u32[]{:S(2)}) copy-start(bf16[512,128]{1,0:T(8,128)(2,1)} %param.7) | copy-start | bytes 393220
  120.3 128.2 %all-gather.6.cloned.1.call-start = ((), (), s32[]{:S(2)}) async-start(), calls=%async_computation.5 | async-start | bytes 4325376 | tf_op jit(solution)/shard_map/all_gather | solution.py:31
  164.3 147.5 %reduce-scatter.6.cloned.1.call-start = ((), (), s32[]{:S(2)}) async-start(), calls=%async_computation.6 | async-start | bytes 1179648 | tf_op jit(solution)/shard_map/reduce_scatter | solution.py:40
  263.8 48.0 %copy-start = (bf16[512,128]{1,0:T(8,128)(2,1)S(1)}, bf16[512,128]{1,0:T(8,128)(2,1)}, u32[]{:S(2)}) copy-start(bf16[512,128]{1,0:T(8,128)(2,1)} %fusion.32) | copy-start | bytes 393220
  269.4 128.2 %all-gather.8.cloned.1.call-start = ((), (), s32[]{:S(2)}) async-start(), calls=%async_computation.7 | async-start | bytes 4325376 | tf_op jit(solution)/shard_map/all_gather | solution.py:31
  313.4 147.3 %reduce-scatter.8.cloned.1.call-start = ((), (), s32[]{:S(2)}) async-start(), calls=%async_computation.8 | async-start | bytes 1179648 | tf_op jit(solution)/shard_map/reduce_scatter | solution.py:40
  412.8 47.9 %copy-start.2 = (bf16[512,128]{1,0:T(8,128)(2,1)S(1)}, bf16[512,128]{1,0:T(8,128)(2,1)}, u32[]{:S(2)}) copy-start(bf16[512,128]{1,0:T(8,128)(2,1)} %fusion.33) | copy-start | bytes 393220
Sparse Core Ops, SparseCore 0:
  10.5 88.9 all-gather.3
  120.4 42.1 reduce-scatter.3
  165.8 82.6 all-gather.5
  269.5 42.2 reduce-scatter.5
  314.8 82.7 all-gather.7
  418.5 42.1 reduce-scatter.7
where the time goes:
time: 471 us; the launch traced here: 469 us
  waiting for transfers between devices  386 us (82%)
  matrix products  32.6 us (7%)
  local copies, waits for them, and re-layouts  29.7 us (6%)
  between operations  14.2 us (3%)
  other arithmetic  6.19 us (1%)
    all_gather x3, waiting for transfers between devices, apply_tiles(): gathered = lax.all_gather(current, 'row', axis=0, tiled=True)  258 us
    reduce_scatter x3, waiting for transfers between devices, apply_tiles(): lax.psum_scatter(term.astype(jnp.bfloat16), 'col', scatter_dimension=0, t...  127 us
    dot_general x3, matrix products, apply_tiles(): jnp.einsum('sij,sjk->sik', tile_data, vec_blocks, preferred_element_type=...  19.7 us
    dot_general x3, local copies, waits for them, and re-layouts, apply_tiles(): jnp.einsum('sij,sjk->sik', tile_data, vec_blocks, preferred_element_type=...  16.5 us
    dot_general x3, matrix products, apply_tiles(): jnp.einsum('ls,sik->lik', onehot, products, precision=lax.Precision.HIGHEST)  12.9 us
  transfers between devices with their start and end apart: 6, of which 6 were waited for; matrix products, arithmetic and copies ran while one was open for 0% of the time, Pallas kernels for 0%

commit v1 on v0

v1 whole, which is shorter than its diff:
```python
import jax
import jax.numpy as jnp
from jax import lax
from jax.experimental import pallas as pl
from jax.experimental.pallas import tpu as pltpu
from jax.sharding import PartitionSpec as P

DEGREE = 3
CENTER = 0.5
MESH = pl.DeviceIdType.MESH

NX, NY, NZ = 4, 8, 4
SLOTS, RB, BLK, PIECE, LANES = 32, 16, 256, 512, 128

CUT = 152
PARTS = ((0, CUT), (CUT, BLK - CUT))


def _messages():
    msgs = []

    def add(rows, link, off, deps):
        msgs.append({"rows": rows, "link": link, "off": off, "deps": tuple(deps)})
        return len(msgs) - 1

    def rows_of(part, first, count):
        lo, n = PARTS[part]
        return (first, count, lo, n)

    def ring(axis, size, part, off, have):
        got = {0: tuple(have)}
        for sign in (1, -1):
            dep = tuple(have)
            for d in range(1, size // 2 + 1):
                o = list(off)
                o[axis] -= sign * (d - 1)
                last = d == size // 2
                rows = rows_of(part, 0 if sign > 0 else 1, 1) if last else rows_of(part, 0, 2)
                m = add(rows, (axis, sign), tuple(o), dep)
                dep = (m,)
                if last:
                    got[size // 2] = got.get(size // 2, ()) + (m,)
                else:
                    got[-sign * d] = (m,)
        return got

    for part, (first, second) in enumerate(((1, 0), (0, 1))):
        sizes = (NX, NY)
        got = ring(first, sizes[first], part, (0, 0), ())
        for d, have in got.items():
            off = [0, 0]
            off[first] = d
            ring(second, sizes[second], part, tuple(off), have)
    return msgs


def _order(msgs, row_us=0.0055, lat=1.7):
    n = len(msgs)

    def size(i):
        return msgs[i]["rows"][1] * msgs[i]["rows"][3]

    users = [[] for _ in range(n)]
    for i, m in enumerate(msgs):
        for d in m["deps"]:
            users[d].append(i)
    tail = [0.0] * n
    for i in reversed(range(n)):
        tail[i] = size(i) * row_us + lat + max((tail[u] for u in users[i]), default=0.0)
    free = {}
    arrive = [None] * n
    start = [None] * n
    left = set(range(n))
    while left:
        best = None
        for i in sorted(left):
            m = msgs[i]
            if any(arrive[d] is None for d in m["deps"]):
                continue
            t = max([free.get(m["link"], 0.0)] + [arrive[d] for d in m["deps"]])
            key = (t, -tail[i], i)
            if best is None or key < best:
                best = key
        t, _, i = best
        start[i] = t
        free[msgs[i]["link"]] = t + size(i) * row_us
        arrive[i] = free[msgs[i]["link"]] + lat
        left.discard(i)
    return sorted(range(n), key=lambda i: (start[i], i)), arrive


MSGS = _messages()
ORDER, ARRIVE = _order(MSGS)
N_MSG = len(MSGS)


def kernel(
    vec_ref, tiles_ref, cols_ref, links_ref, out_ref,
    g0, g1, g2, tiles, seg, xs, xr, zs, zr,
    in_sem, gs_sem, gr_sem, xs_sem, xr_sem, zs_sem, zr_sem,
):
    gathered = (g0, g1, g2)
    row = lax.axis_index("row")
    col = lax.axis_index("col")
    x, y = row // NY, row % NY
    zi, core = col // 2, col % 2

    def row_at(dx, dy):
        return ((x + dx + NX) % NX) * NY + (y + dy + NY) % NY

    links = {
        (0, 1): row_at(1, 0), (0, -1): row_at(-1, 0), (1, 1): row_at(0, 1), (1, -1): row_at(0, -1),
    }
    z_up = ((zi + 1) % NZ) * 2 + core
    z_down = ((zi + NZ - 1) % NZ) * 2 + core
    mate = zi * 2 + 1 - core

    tile_copy = pltpu.make_async_copy(tiles_ref, tiles, in_sem.at[0])
    own = pl.ds(row * 2, 2)
    vec_copy = pltpu.make_async_copy(vec_ref, g0.at[own], in_sem.at[1])
    vec_copy.start()
    tile_copy.start()

    barrier = pltpu.get_barrier_semaphore()
    for to in links.values():
        pl.semaphore_signal(barrier, inc=1, device_id={"row": to}, device_id_type=MESH)
    for to in (z_up, z_down, mate):
        pl.semaphore_signal(barrier, inc=1, device_id={"col": to}, device_id_type=MESH)
    seg[SLOTS] = jnp.zeros((BLK, LANES), jnp.float32)
    pl.semaphore_wait(barrier, 7)
    vec_copy.wait()

    def region(k, off, rows):
        first, count, lo, n = rows
        return gathered[k].at[pl.ds(row_at(*off) * 2 + first, count), pl.ds(lo, n)]

    def message(k, i, receive):
        m = MSGS[i]
        off = list(m["off"])
        if receive:
            off[m["link"][0]] -= m["link"][1]
        ref = region(k, off, m["rows"])
        return pltpu.make_async_remote_copy(
            src_ref=ref, dst_ref=ref, send_sem=gs_sem.at[k * N_MSG + i], recv_sem=gr_sem.at[k * N_MSG + i],
            device_id={"row": links[m["link"]]}, device_id_type=MESH,
        )

    def gather(k):
        done = set()
        for i in ORDER:
            for d in MSGS[i]["deps"]:
                if d not in done:
                    message(k, d, True).wait_recv()
                    done.add(d)
            message(k, i, False).start()
        for i in sorted(range(N_MSG), key=lambda i: ARRIVE[i]):
            if i not in done:
                message(k, i, True).wait_recv()

    def compute(k):
        g = gathered[k]

        def step(s, carry):
            v = g[cols_ref[0, 0, s]]
            seg[s] = jnp.dot(tiles[s], v, preferred_element_type=jnp.float32) + seg[links_ref[s]]
            return carry

        lax.fori_loop(0, SLOTS, step, 0)

    def block(l):
        return seg[links_ref[SLOTS + l]]

    def x_copy(k, t):
        return pltpu.make_async_remote_copy(
            src_ref=xs.at[k, t], dst_ref=xr.at[k, t], send_sem=xs_sem.at[k * NZ + t], recv_sem=xr_sem.at[k * NZ + t],
            device_id={"col": mate}, device_id_type=MESH,
        )

    def z_copy(k, i, to):
        return pltpu.make_async_remote_copy(
            src_ref=zs.at[k, i], dst_ref=zr.at[k, i], send_sem=zs_sem.at[k * 6 + i], recv_sem=zr_sem.at[k * 6 + i],
            device_id={"col": to}, device_id_type=MESH,
        )

    def scatter(k):
        targets = ((zi + 2) % NZ, (zi + 1) % NZ, (zi + NZ - 1) % NZ, zi)
        for t, z in enumerate(targets):
            for h in range(2):
                xs[k, t, pl.ds(h * BLK, BLK), :] = block((z * 2 + 1 - core) * 2 + h).astype(jnp.bfloat16)
            x_copy(k, t).start()

        def mine(t, h):
            return block((targets[t] * 2 + core) * 2 + h) + xr[k, t, pl.ds(h * BLK, BLK), :].astype(jnp.float32)

        def send(i, value, to):
            zs[k, i] = value.astype(jnp.bfloat16)
            z_copy(k, i, to).start()

        x_copy(k, 0).wait_recv()
        send(0, mine(0, 0), z_up)
        send(1, mine(0, 1), z_down)
        x_copy(k, 1).wait_recv()
        send(2, mine(1, 1), z_up)
        x_copy(k, 2).wait_recv()
        send(3, mine(2, 0), z_down)
        z_copy(k, 0, z_up).wait_recv()
        send(4, mine(1, 0) + zr[k, 0].astype(jnp.float32), z_up)
        z_copy(k, 1, z_down).wait_recv()
        send(5, mine(2, 1) + zr[k, 1].astype(jnp.float32), z_down)
        x_copy(k, 3).wait_recv()
        z_copy(k, 3, z_down).wait_recv()
        z_copy(k, 2, z_up).wait_recv()
        for h, i in ((0, 4), (1, 5)):
            z_copy(k, i, z_up).wait_recv()
            applied = mine(3, h) + zr[k, i].astype(jnp.float32) + zr[k, 3 - h].astype(jnp.float32)
            here = row * 2 + h
            now = gathered[k][here].astype(jnp.float32)
            value = applied - CENTER * now
            if k == 0:
                value = 0.5 * value
            else:
                value = value - gathered[k - 1][here].astype(jnp.float32)
            value = value.astype(jnp.bfloat16)
            if k == DEGREE - 1:
                out_ref[h] = value
            else:
                gathered[k + 1][here] = value

    for k in range(DEGREE):
        gather(k)
        if k == 0:
            tile_copy.wait()
        compute(k)
        scatter(k)
    for k in range(DEGREE):
        for i in range(N_MSG):
            message(k, i, False).wait_send()
        for t in range(NZ):
            x_copy(k, t).wait_send()
        for i in range(6):
            z_copy(k, i, z_up).wait_send()


def on_device(vectors, tile_blocks, block_rows, block_cols, counts):
    slot = jnp.arange(SLOTS, dtype=jnp.int32)
    rows = block_rows[0, 0]
    wanted = jnp.concatenate([rows, jnp.arange(RB, dtype=jnp.int32)])
    before = jnp.concatenate([slot, jnp.full((RB,), SLOTS, jnp.int32)])
    hit = (rows[None, :] == wanted[:, None]) & (slot[None, :] < jnp.minimum(before, counts[0, 0])[:, None])
    links = jnp.max(jnp.where(hit, slot[None, :], -1), axis=1)
    links = jnp.where(links < 0, SLOTS, links)
    any_spec = pl.BlockSpec(memory_space=pl.ANY)
    smem = pl.BlockSpec(memory_space=pltpu.SMEM)
    dma = pltpu.SemaphoreType.DMA
    return pl.pallas_call(
        kernel,
        out_shape=jax.ShapeDtypeStruct((2, BLK, LANES), jnp.bfloat16),
        in_specs=[any_spec, any_spec, smem, smem],
        out_specs=pl.BlockSpec(memory_space=pltpu.VMEM),
        scratch_shapes=[
            pltpu.VMEM((NX * NY * 2, BLK, LANES), jnp.bfloat16),
            pltpu.VMEM((NX * NY * 2, BLK, LANES), jnp.bfloat16),
            pltpu.VMEM((NX * NY * 2, BLK, LANES), jnp.bfloat16),
            pltpu.VMEM((SLOTS, BLK, BLK), jnp.bfloat16),
            pltpu.VMEM((SLOTS + 1, BLK, LANES), jnp.float32),
            pltpu.VMEM((DEGREE, NZ, PIECE, LANES), jnp.bfloat16),
            pltpu.VMEM((DEGREE, NZ, PIECE, LANES), jnp.bfloat16),
            pltpu.VMEM((DEGREE, 6, BLK, LANES), jnp.bfloat16),
            pltpu.VMEM((DEGREE, 6, BLK, LANES), jnp.bfloat16),
            dma((2,)),
            dma((DEGREE * N_MSG,)),
            dma((DEGREE * N_MSG,)),
            dma((DEGREE * NZ,)),
            dma((DEGREE * NZ,)),
            dma((DEGREE * 6,)),
            dma((DEGREE * 6,)),
        ],
        compiler_params=pltpu.CompilerParams(collective_id=0, has_side_effects=True),
        name="filter",
    )(vectors.reshape(2, BLK, LANES), tile_blocks[0, 0], block_cols, links).reshape(PIECE, LANES)


def solution(mesh):
    return jax.shard_map(
        on_device,
        mesh=mesh,
        in_specs=(
            P(("row", "col"), "vec"),
            P("row", "col", None, None, None),
            P("row", "col", None),
            P("row", "col", None),
            P("row", "col"),
        ),
        out_specs=P(("row", "col"), "vec"),
        check_vma=False,
    )
```

time: 471 us -> 158 us (0.34)
  waiting for transfers between devices: 386 us -> 0 us
  Pallas kernels: 0 us -> 154 us
  matrix products: 32.6 us -> 0 us
  local copies, waits for them, and re-layouts: 29.7 us -> 1.57 us
  between operations: 14.2 us -> 0.67 us
    all_gather x3 -> x0, waiting for transfers between devices: 258 us -> none  [apply_tiles(): gathered = lax.all_gather(current, 'row', axis=0, tiled=True)]
    pallas_call x0 -> x1, Pallas kernels: none -> 154 us  [on_device(): pl.pallas_call(kernel, out_shape=jax.ShapeDtypeStruct((2, BLK, LANES), jn...]
    reduce_scatter x3 -> x0, waiting for transfers between devices: 127 us -> none  [apply_tiles(): lax.psum_scatter(term.astype(jnp.bfloat16), 'col', scatter_dimension=0, t...]
    dot_general x6 -> x0, matrix products: 32.6 us -> none  [the longest x3 19.7 us: apply_tiles(): jnp.einsum('sij,sjk->sik', tile_data, vec_blocks, preferred_element_type=...]
    dot_general x3 -> x0, local copies, waits for them, and re-layouts: 16.5 us -> none  [apply_tiles(): jnp.einsum('sij,sjk->sik', tile_data, vec_blocks, preferred_element_type=...]
    gather x3 -> x0, local copies, waits for them, and re-layouts: 9.41 us -> none  [apply_tiles(): jnp.take(gathered.reshape(n_row * piece_blocks, block_size, width), slot_...]
    convert_element_type x4 -> x0, other arithmetic: 4.86 us -> none  [the longest x2 3.24 us: on_device(): following = (2.0 * (applied - center_value * current.astype(jnp.float32))...]
  transfers between devices with their start and end apart: 6 -> 0, of which waited for: 6 -> 0; matrix products, arithmetic and copies ran while one was open for 0% -> 0% of each run, Pallas kernels for 0% -> 0%
where the time goes in v1:
time: 158 us
  Pallas kernels  154 us (97%)
  other arithmetic  2.01 us (1%)
    pallas_call x1, Pallas kernels, on_device(): pl.pallas_call(kernel, out_shape=jax.ShapeDtypeStruct((2, BLK, LANES), jn...  154 us

profile of v1, /device:TPU:1, one launch (start us, length us, event | category | flops | bytes accessed | tf_op | source)
XLA Modules:
  0.0 158.1 jit_solution(3644155294501428440)
XLA Ops:
  0.7 0.8 pad_add_fusion
  1.4 0.7 select_reduce_fusion
  2.2 0.5 compare_select_fusion.links_ref
  2.7 153.8 %filter.1 = bf16[2,256,128]{2,1,0:T(8,128)(2,1)} custom-call(bf16[2,256,128]{2,1,0:T(8,128)(2,1)} %bitcast.8, bf16[32,256,256]{2,1,0:T(8,128)(2,1)} %bitcast.6, s32[1,1,32]{2,1,0:T(1,128)} %cols_ref.1, s32[48]{0:T(128)} %compare_select_fusion.links_ref), custom_call_target="tpu_custom_call" | custom-call | tf_op jit(solution)/shard_map/filter/pallas_call | solution.py:255
  156.5 1.6 copy.8
  (1 shorter events, 0.0 us)
